TPU v7x, 256 devices: a whole 4x4x8 slice. The times are simulated.
256 devices in a mesh: row: 16 (over z, core), col: 16 (over y, x).
Axes of the slice: x: 4, y: 4, z: 8, core: 2. Of those that a mesh axis runs over, the one named last changes fastest.
Arguments:
- inverse: float32 [5, 16, 5, 16, 256, 256], P(None, 'row', None, 'col')
- struct_first: int32 [32], replicated, may hold values from 0 to 79, as said below
- struct_second: int32 [16], replicated, may hold values from 0 to 79, as said below
- factor_first: float32 [32, 256, 256], P('row'), may hold values from -0.25 to 0.25
- factor_second: float32 [16, 256, 256], P('row'), may hold values from -0.25 to 0.25
- link_factor: float32 [256, 256], replicated, may hold values from -0.375 to 0.375
- dinv_first: float32 [256, 256], replicated, may hold values from -6 to 6
- dinv_second: float32 [256, 256], replicated, may hold values from -6 to 6
Outputs:
- column_first: float32 [5, 16, 256, 256], P(None, 'row', None, 'col')
- diag_first: float32 [256, 256], P(None, 'col')
- column_second: float32 [5, 16, 256, 256], P(None, 'row', None, 'col')
- link_second: float32 [256, 256], P(None, 'col')
- diag_second: float32 [256, 256], P(None, 'col')
Inputs may be any that keep to these rules, and one draw needn't show every extreme that they name: `struct_first`: distinct tile ids. `struct_second`: distinct tile ids, each of them also in struct_first.
All inputs are finite; a program needn't handle non-finite values.
Results may differ from a plain program's by a relative error of at most 0.0001.
Values sent between devices are 32-bit elements; how exact they have to be, the bound alone decides.
A program may use at most 128 MiB of HBM per device.

v0:
```python
import jax
import jax.numpy as jnp
from jax import lax
from jax.sharding import PartitionSpec as P

PRECISE = lax.Precision.HIGHEST


def body(
    inverse,
    struct_first,
    struct_second,
    factor_first,
    factor_second,
    link_factor,
    dinv_first,
    dinv_second,
):
    grid_rows = lax.axis_size("row")
    grid_cols = lax.axis_size("col")
    my_row = lax.axis_index("row")
    my_col = lax.axis_index("col")
    tile_rows, _, tile_cols, _, extent, _ = inverse.shape
    local_inv = inverse.reshape(tile_rows, tile_cols, extent, extent)
    col_width = extent // grid_cols
    offset = my_col * col_width
    col_tiles = jnp.arange(tile_cols, dtype=jnp.int32) * grid_cols + my_col
    row_tiles = jnp.arange(tile_rows, dtype=jnp.int32) * grid_rows + my_row

    def route(factor, tile_ids):
        block_in = lax.all_gather(factor, "row", axis=0, tiled=True)
        pick_col = (tile_ids[None, :] == col_tiles[:, None]).astype(jnp.float32)
        pick_row = (tile_ids[None, :] == row_tiles[:, None]).astype(jnp.float32)
        col_sel = jnp.einsum("bj,jxy->bxy", pick_col, block_in, precision=PRECISE)
        row_sel = jnp.einsum("aj,jxy->axy", pick_row, block_in, precision=PRECISE)
        return (col_sel, row_sel)

    def reduce_cols(stacked):
        summed = lax.psum(stacked, "col")
        return lax.dynamic_slice_in_dim(summed, offset, col_width, 2)

    col_first, row_first = route(factor_first, struct_first)
    product_first = jnp.einsum("abxy,byz->axz", local_inv, col_first, precision=PRECISE)
    panel_first = reduce_cols(product_first)
    owned_first = jnp.any(row_tiles[:, None] == struct_first[None, :], axis=1).astype(jnp.float32)
    column_first = -owned_first[:, None, None] * panel_first
    diag_terms = jnp.einsum("axy,axz->yz", row_first, panel_first, precision=PRECISE)
    diag_first = lax.dynamic_slice_in_dim(dinv_first, offset, col_width, 1) + lax.psum(
        diag_terms, "row"
    )
    col_second, row_second = route(factor_second, struct_second)
    link_rows = lax.dynamic_slice_in_dim(link_factor, offset, col_width, 0)
    product_second = jnp.einsum("abxy,byz->axz", local_inv, col_second, precision=PRECISE)
    product_second = product_second + jnp.einsum(
        "axw,wz->axz", column_first, link_rows, precision=PRECISE
    )
    link_term = jnp.dot(
        diag_first, link_rows, precision=PRECISE, preferred_element_type=jnp.float32
    )
    reduced = reduce_cols(jnp.concatenate([product_second, link_term[None]], axis=0))
    panel_second = reduced[:tile_rows]
    join_share = reduced[tile_rows]
    owned_second = jnp.any(row_tiles[:, None] == struct_second[None, :], axis=1).astype(jnp.float32)
    column_second = -owned_second[:, None, None] * panel_second
    turned_part = jnp.einsum("axw,axz->wz", column_first, row_second, precision=PRECISE)
    second_terms = jnp.einsum("axy,axz->yz", row_second, panel_second, precision=PRECISE)
    turned_sum, second_sum = lax.psum((turned_part, second_terms), "row")
    turned = lax.all_to_all(turned_sum, "col", split_axis=1, concat_axis=0, tiled=True)
    joined = turned + join_share
    link_second = -joined
    diag_second = lax.dynamic_slice_in_dim(dinv_second, offset, col_width, 1) + second_sum
    diag_second = diag_second + jnp.dot(
        link_factor.T, joined, precision=PRECISE, preferred_element_type=jnp.float32
    )
    out_shape = (tile_rows, 1, extent, col_width)
    return (
        column_first.reshape(out_shape),
        diag_first,
        column_second.reshape(out_shape),
        link_second,
        diag_second,
    )


def solution(mesh):
    placed = (
        P(None, "row", None, "col", None, None),
        P(),
        P(),
        P("row", None, None),
        P("row", None, None),
        P(),
        P(),
        P(),
    )
    return jax.shard_map(
        body,
        mesh=mesh,
        in_specs=placed,
        out_specs=(
            P(None, "row", None, "col"),
            P(None, "col"),
            P(None, "row", None, "col"),
            P(None, "col"),
            P(None, "col"),
        ),
        check_vma=False,
    )
```

profile of v0, /device:TPU:2, one launch (start us, length us, event | category | flops | bytes accessed | tf_op | source)
XLA Modules:
  0.0 435.4 jit_solution(15003734028828694786)
XLA Ops:
  10.7 58.0 %all-gather.3.cloned.1.call-done = f32[32,256,256]{2,1,0:T(8,128)} async-done(((f32[2,256,256]{2,1,0:T(8,128)}), f32[32,256,256]{2,1,0:T(8,128)}) %all-gather.3.cloned.1.call-update) | async-done | bytes 8388624 | tf_op jit(solution)/shard_map/all_gather | solution.py:31
  68.7 10.6 %fusion.2 = f32[5,256,256]{2,0,1:T(8,128)S(1)} fusion(f32[32,256,256]{2,1,0:T(8,128)} %all-gather.3.cloned.1.call-done, s32[32]{0:T(128)} %param.9, s32[5]{0:T(128)S(1)} %fusion.62), kind=kOutput, calls=%fused_computation.2 | convolution fusion | flops 125829280 | bytes 9699476 | tf_op jit(solution)/shard_map/bj,jxy->bxy/dot_general | solution.py:34
  79.3 1.5 copy.35
  80.8 9.9 %fusion.12 = f32[5,256,256]{1,2,0:T(8,128)} fusion(f32[5,1,5,1,256,256]{5,4,3,2,1,0:T(8,128)} %param.8, f32[5,256,256]{1,2,0:T(8,128)} %copy.35), kind=kOutput, calls=%fused_computation.13 | convolution fusion | flops 5033164800 | bytes 9175040 | tf_op jit(solution)/shard_map/abxy,byz->axz/dot_general | solution.py:43
  90.8 10.8 %all-reduce.6.cloned.1.call-start = ((), (), s32[]{:S(2)}) async-start(), calls=%async_computation.4 | async-start | bytes 3145728 | tf_op jit(solution)/shard_map/psum | solution.py:39
  101.6 9.4 %all-gather.5.cloned.1.call-done = f32[16,256,256]{2,1,0:T(8,128)} async-done(((f32[1,256,256]{2,1,0:T(8,128)}), f32[16,256,256]{2,1,0:T(8,128)}) %all-gather.5.cloned.1.call-update) | async-done | bytes 4194320 | tf_op jit(solution)/shard_map/all_gather | solution.py:31
  111.0 5.8 %fusion.10 = f32[5,256,256]{2,0,1:T(8,128)S(1)} fusion(f32[16,256,256]{2,1,0:T(8,128)} %all-gather.5.cloned.1.call-done, s32[16]{0:T(128)S(1)} %copy-done.4, s32[5]{0:T(128)S(1)} %fusion.62), kind=kOutput, calls=%fused_computation.10 | convolution fusion | flops 62914640 | bytes 5505108 | tf_op jit(solution)/shard_map/bj,jxy->bxy/dot_general | solution.py:34
  116.8 1.5 copy.40
  118.3 10.0 %fusion.15 = f32[5,256,256]{1,2,0:T(8,128)} fusion(f32[5,1,5,1,256,256]{5,4,3,2,1,0:T(8,128)} %param.8, f32[5,256,256]{1,2,0:T(8,128)} %copy.40), kind=kOutput, calls=%fused_computation.14 | convolution fusion | flops 5033164800 | bytes 9175040 | tf_op jit(solution)/shard_map/abxy,byz->axz/dot_general | solution.py:53
  128.3 10.7 %fusion = f32[5,256,256]{2,0,1:T(8,128)S(1)} fusion(f32[32,256,256]{2,1,0:T(8,128)} %all-gather.3.cloned.1.call-done, s32[32]{0:T(128)S(1)} %copy-done.3, s32[5]{0:T(128)S(1)} %fusion.63), kind=kOutput, calls=%fused_computation | convolution fusion | flops 125829280 | bytes 9699476 | tf_op jit(solution)/shard_map/aj,jxy->axy/dot_general | solution.py:35
  139.0 71.3 %all-reduce.4.cloned.1.call-done = f32[5,256,256]{1,2,0:T(8,128)} async-done(((f32[5,256,256]{1,2,0:T(8,128)}), f32[5,256,256]{1,2,0:T(8,128)}) %all-reduce.4.cloned.1.call-update) | async-done | bytes 1310736 | tf_op jit(solution)/shard_map/psum | solution.py:39
  210.4 1.9 fusion.22
  212.3 46.3 %psum.36 = f32[256,16]{0,1:T(8,128)S(1)} all-reduce(f32[256,16]{0,1:T(8,128)S(1)} %fusion.22), channel_id=1, replica_groups=mesh['row'=16,'col'=16] {'row'}, use_global_device_ids=true, to_apply=%region_2.0 | all-reduce | flops 4096 | bytes 32768 | tf_op jit(solution)/shard_map/psum | solution.py:48
  259.0 2.6 convolution_add_fusion
  264.2 5.8 %fusion.8 = f32[5,256,256]{2,0,1:T(8,128)S(1)} fusion(f32[16,256,256]{2,1,0:T(8,128)} %all-gather.5.cloned.1.call-done, s32[16]{0:T(128)S(1)} %copy-done.4, s32[5]{0:T(128)S(1)} %fusion.63), kind=kOutput, calls=%fused_computation.8 | convolution fusion | flops 62914640 | bytes 5505108 | tf_op jit(solution)/shard_map/aj,jxy->axy/dot_general | solution.py:35
  270.0 1.6 fusion.31
  271.6 3.2 fusion.27
  274.9 86.3 %all-reduce.6.cloned.1.call-done = f32[6,256,256]{1,2,0:T(8,128)} async-done(((f32[6,256,256]{1,2,0:T(8,128)}), f32[6,256,256]{1,2,0:T(8,128)}) %all-reduce.6.cloned.1.call-update) | async-done | bytes 1572880 | tf_op jit(solution)/shard_map/psum | solution.py:39
  361.2 1.9 convolution_bitcast_fusion.1
  363.1 48.2 %all-reduce = (f32[16,16,16]{0,2,1:T(8,128)S(1)}, f32[256,16]{0,1:T(8,128)S(1)}) all-reduce(f32[16,16,16]{0,2,1:T(8,128)S(1)} %bitcast.78, f32[256,16]{0,1:T(8,128)S(1)} %convolution_bitcast_fusion.1), channel_id=1, replica_groups=mesh['row'=16,'col'=16] {'row'}, use_global_device_ids=true, to_apply=%region_5.0 | all-reduce | flops 8192 | bytes 65536 | tf_op jit(solution)/shard_map/psum | solution.py:67
  412.0 5.9 %all-to-all-start = ((f32[16,1,256]{2,1,0:T(1,128)}), f32[16,1,256]{2,1,0:T(1,128)S(1)}, u32[]{:S(2)}, u32[]{:S(2)}) async-start(f32[16,1,256]{2,1,0:T(1,128)} %reshape.57), calls=%async_computation | async-start | bytes 32768 | tf_op jit(solution)/shard_map/all_to_all | solution.py:68
  417.9 1.6 multiply_bitcast_fusion
  419.5 4.6 %all-to-all-done = f32[16,1,256]{2,1,0:T(1,128)S(1)} async-done(((f32[16,1,256]{2,1,0:T(1,128)}), f32[16,1,256]{2,1,0:T(1,128)S(1)}, u32[]{:S(2)}, u32[]{:S(2)}) %all-to-all-start) | async-done | bytes 16416 | tf_op jit(solution)/shard_map/all_to_all | solution.py:68
  426.9 1.6 fusion.25
  (38 shorter events, 9.9 us)
Async XLA Ops:
  7.2 251.4 %copy-start = (f32[256,256]{1,0:T(8,128)S(1)}, f32[256,256]{1,0:T(8,128)}, u32[]{:S(2)}) copy-start(f32[256,256]{1,0:T(8,128)} %param.13) | copy-start | bytes 786436
  7.2 61.5 %all-gather.3.cloned.1.call-start = ((), (), s32[]{:S(2)}) async-start(), calls=%async_computation.1 | async-start | bytes 8912896 | tf_op jit(solution)/shard_map/all_gather | solution.py:31
  7.9 103.0 %all-gather.5.cloned.1.call-start = ((), (), s32[]{:S(2)}) async-start(), calls=%async_computation.3 | async-start | bytes 4456448 | tf_op jit(solution)/shard_map/all_gather | solution.py:31
  8.7 201.7 %all-reduce.4.cloned.1.call-start = ((), (), s32[]{:S(2)}) async-start(), calls=%async_computation.2 | async-start | bytes 2621440 | tf_op jit(solution)/shard_map/psum | solution.py:39
  80.8 30.1 %copy-start.4 = (s32[16]{0:T(128)S(1)}, s32[16]{0:T(128)}, u32[]{:S(2)}) copy-start(s32[16]{0:T(128)} %param.10) | copy-start | bytes 196
  90.8 270.4 %all-reduce.6.cloned.1.call-start = ((), (), s32[]{:S(2)}) async-start(), calls=%async_computation.4 | async-start | bytes 3145728 | tf_op jit(solution)/shard_map/psum | solution.py:39
  118.3 10.0 %copy-start.3 = (s32[32]{0:T(128)S(1)}, s32[32]{0:T(128)}, u32[]{:S(2)}) copy-start(s32[32]{0:T(128)} %param.9) | copy-start | bytes 388
  258.5 4.3 copy-start.1
  262.9 1.0 copy-start.2
  412.0 12.1 %all-to-all-start = ((f32[16,1,256]{2,1,0:T(1,128)}), f32[16,1,256]{2,1,0:T(1,128)S(1)}, u32[]{:S(2)}, u32[]{:S(2)}) async-start(f32[16,1,256]{2,1,0:T(1,128)} %reshape.57), calls=%async_computation | async-start | bytes 32768 | tf_op jit(solution)/shard_map/all_to_all | solution.py:68
Sparse Core Ops, SparseCore 0:
  9.8 58.7 all-gather.2
  70.5 40.4 all-gather.4
  114.2 96.1 all-reduce.3
  263.0 98.1 all-reduce.5
where the time goes:
time: 444 us; the launch traced here: 435 us
  waiting for transfers between devices  231 us (52%)
  blocking collectives  94.4 us (21%)
  matrix products  64.5 us (15%)
  starting transfers between devices  16.8 us (4%)
  between operations  14.3 us (3%)
  other arithmetic  7.53 us (2%)
  local copies, waits for them, and re-layouts  6.73 us (2%)
    psum x2, waiting for transfers between devices, reduce_cols(): summed = lax.psum(stacked, 'col')  158 us
    all_gather x2, waiting for transfers between devices, route(): block_in = lax.all_gather(factor, 'row', axis=0, tiled=True)  67.4 us
    psum x1, blocking collectives, body(): turned_sum, second_sum = lax.psum((turned_part, second_terms), 'row')  48.2 us
    psum x1, blocking collectives, body(): lax.psum(diag_terms, 'row')  46.3 us
    dot_general x2, matrix products, route(): row_sel = jnp.einsum('aj,jxy->axy', pick_row, block_in, precision=PRECISE)  16.6 us
    dot_general x2, matrix products, route(): col_sel = jnp.einsum('bj,jxy->bxy', pick_col, block_in, precision=PRECISE)  16.5 us
    psum x2, starting transfers between devices, reduce_cols(): summed = lax.psum(stacked, 'col')  10.8 us
    dot_general x1, matrix products, body(): jnp.einsum('abxy,byz->axz', local_inv, col_second, precision=PRECISE)  9.96 us
  transfers between devices with their start and end apart: 5, of which 5 were waited for; matrix products, arithmetic and copies ran while one was open for 15% of the time, Pallas kernels for 0%

commit v1 on v0

--- a/solution.py
+++ b/solution.py
@@ -4,6 +4,16 @@
 from jax.sharding import PartitionSpec as P
 
 PRECISE = lax.Precision.HIGHEST
+
+
+def see_records_for(tile_in):
+    amount_of = jax.lax.axis_size("col")
+    high, v1 = (tile_in, 0)
+    while 1 << v1 < amount_of:
+        parts_out = jax.lax.ppermute(high, "col", [(s, s ^ 1 << v1) for s in range(amount_of)])
+        high = high + parts_out
+        v1 = v1 + 1
+    return high
 
 
 def body(
@@ -36,7 +46,7 @@
         return (col_sel, row_sel)
 
     def reduce_cols(stacked):
-        summed = lax.psum(stacked, "col")
+        summed = see_records_for(stacked)
         return lax.dynamic_slice_in_dim(summed, offset, col_width, 2)
 
     col_first, row_first = route(factor_first, struct_first)

time: 444 us -> 502 us (1.13)
  waiting for transfers between devices: 231 us -> 271 us
  starting transfers between devices: 16.8 us -> 36.4 us
  matrix products: 64.5 us -> 57.6 us
  blocking collectives: 94.4 us -> 101 us
    ppermute x0 -> x8, waiting for transfers between devices: none -> 204 us  [see_records_for(): jax.lax.ppermute(high, 'col', [(s, s ^ 1 << v1) for s in range(amount_of)])]
    psum x2 -> x0, waiting for transfers between devices: 158 us -> none  [reduce_cols(): summed = lax.psum(stacked, 'col')]
    ppermute x0 -> x8, starting transfers between devices: none -> 29 us  [see_records_for(): jax.lax.ppermute(high, 'col', [(s, s ^ 1 << v1) for s in range(amount_of)])]
    psum x2 -> x0, starting transfers between devices: 10.8 us -> none  [reduce_cols(): summed = lax.psum(stacked, 'col')]
    all_gather x2, waiting for transfers between devices: 67.4 us -> 60 us  [route(): block_in = lax.all_gather(factor, 'row', axis=0, tiled=True)]
    psum x1, blocking collectives: 48.2 us -> 54.8 us  [body(): turned_sum, second_sum = lax.psum((turned_part, second_terms), 'row')]
  transfers between devices with their start and end apart: 5 -> 11, of which waited for: 5 -> 10; matrix products, arithmetic and copies ran while one was open for 15% -> 12% of each run, Pallas kernels for 0% -> 0%
where the time goes in v1:
time: 502 us; the launch traced here: 493 us
  waiting for transfers between devices  271 us (54%)
  blocking collectives  101 us (20%)
  matrix products  57.6 us (11%)
  starting transfers between devices  36.4 us (7%)
  between operations  14.7 us (3%)
  other arithmetic  7.38 us (1%)
    ppermute x8, waiting for transfers between devices, see_records_for(): jax.lax.ppermute(high, 'col', [(s, s ^ 1 << v1) for s in range(amount_of)])  204 us
    all_gather x2, waiting for transfers between devices, route(): block_in = lax.all_gather(factor, 'row', axis=0, tiled=True)  60 us
    psum x1, blocking collectives, body(): turned_sum, second_sum = lax.psum((turned_part, second_terms), 'row')  54.8 us
    psum x1, blocking collectives, body(): lax.psum(diag_terms, 'row')  45.9 us
    ppermute x8, starting transfers between devices, see_records_for(): jax.lax.ppermute(high, 'col', [(s, s ^ 1 << v1) for s in range(amount_of)])  29 us
    dot_general x2, matrix products, route(): row_sel = jnp.einsum('aj,jxy->axy', pick_row, block_in, precision=PRECISE)  16.6 us
    dot_general x2, matrix products, route(): col_sel = jnp.einsum('bj,jxy->bxy', pick_col, block_in, precision=PRECISE)  16.5 us
  transfers between devices with their start and end apart: 11, of which 10 were waited for; matrix products, arithmetic and copies ran while one was open for 12% of the time, Pallas kernels for 0%

profile of v1, /device:TPU:2, one launch (start us, length us, event | category | flops | bytes accessed | tf_op | source)
XLA Modules:
  0.0 492.9 jit_solution(6123610381355474014)
XLA Ops:
  8.7 60.0 %all-gather.3.cloned.1.call-done = f32[32,256,256]{2,1,0:T(8,128)} async-done(((f32[2,256,256]{2,1,0:T(8,128)}), f32[32,256,256]{2,1,0:T(8,128)}) %all-gather.3.cloned.1.call-update) | async-done | bytes 8388624 | tf_op jit(solution)/shard_map/all_gather | solution.py:41
  68.6 10.6 %fusion.2 = f32[5,256,256]{2,0,1:T(8,128)S(1)} fusion(f32[32,256,256]{2,1,0:T(8,128)} %all-gather.3.cloned.1.call-done, s32[32]{0:T(128)} %param.9, s32[5]{0:T(128)S(1)} %fusion.58), kind=kOutput, calls=%fused_computation.2 | convolution fusion | flops 125829280 | bytes 9699476 | tf_op jit(solution)/shard_map/bj,jxy->bxy/dot_general | solution.py:44
  80.8 8.9 %fusion.12 = f32[5,256,256]{1,2,0:T(8,128)S(1)} fusion(f32[5,1,5,1,256,256]{5,4,3,2,1,0:T(8,128)} %param.8, f32[5,256,256]{1,2,0:T(8,128)} %copy.31), kind=kOutput, calls=%fused_computation.13 | convolution fusion | flops 5033164800 | bytes 9175040 | tf_op jit(solution)/shard_map/abxy,byz->axz/dot_general | solution.py:53
  90.3 30.4 %collective-permute-done = f32[5,256,256]{1,2,0:T(8,128)S(1)} collective-permute-done((f32[5,256,256]{1,2,0:T(8,128)S(1)}, f32[5,256,256]{1,2,0:T(8,128)S(1)}, u32[]{:S(2)}, u32[]{:S(2)}) %collective-permute-start) | collective-permute-done | bytes 1310752 | tf_op jit(solution)/shard_map/ppermute | solution.py:13
  120.9 13.9 %collective-permute-start.1 = (f32[5,256,256]{1,2,0:T(8,128)S(1)}, f32[5,256,256]{1,2,0:T(8,128)S(1)}, u32[]{:S(2)}, u32[]{:S(2)}) collective-permute-start(f32[5,256,256]{1,2,0:T(8,128)S(1)} %add.76), channel_id=1, source_target_pairs={{0,2},{1,3},{2,0},{3,1},{4,6},{5,7},{6,4},{7,5},{8,10},{9,11},{10,... | collective-permute-start | bytes 3932168 | tf_op jit(solution)/shard_map/ppermute | solution.py:13
  134.8 29.5 %collective-permute-done.1 = f32[5,256,256]{1,2,0:T(8,128)S(1)} collective-permute-done((f32[5,256,256]{1,2,0:T(8,128)S(1)}, f32[5,256,256]{1,2,0:T(8,128)S(1)}, u32[]{:S(2)}, u32[]{:S(2)}) %collective-permute-start.1) | collective-permute-done | bytes 1310752 | tf_op jit(solution)/shard_map/ppermute | solution.py:13
  166.4 27.3 %collective-permute-done.2 = f32[5,256,256]{1,2,0:T(8,128)S(1)} collective-permute-done((f32[5,256,256]{1,2,0:T(8,128)S(1)}, f32[5,256,256]{1,2,0:T(8,128)S(1)}, u32[]{:S(2)}, u32[]{:S(2)}) %collective-permute-start.2) | collective-permute-done | bytes 1310752 | tf_op jit(solution)/shard_map/ppermute | solution.py:13
  195.1 3.0 collective-permute-start.3
  198.1 5.8 %fusion.10 = f32[5,256,256]{2,0,1:T(8,128)S(1)} fusion(f32[16,256,256]{2,1,0:T(8,128)} %all-gather.5.cloned.1.call-done, s32[16]{0:T(128)S(1)} %copy-done.5, s32[5]{0:T(128)S(1)} %fusion.58), kind=kOutput, calls=%fused_computation.10 | convolution fusion | flops 62914640 | bytes 5505108 | tf_op jit(solution)/shard_map/bj,jxy->bxy/dot_general | solution.py:44
  205.4 8.9 %fusion.15 = f32[5,256,256]{1,2,0:T(8,128)S(1)} fusion(f32[5,1,5,1,256,256]{5,4,3,2,1,0:T(8,128)} %param.8, f32[5,256,256]{1,2,0:T(8,128)} %copy.36), kind=kOutput, calls=%fused_computation.14 | convolution fusion | flops 5033164800 | bytes 9175040 | tf_op jit(solution)/shard_map/abxy,byz->axz/dot_general | solution.py:63
  214.3 10.6 %fusion = f32[5,256,256]{2,0,1:T(8,128)S(1)} fusion(f32[32,256,256]{2,1,0:T(8,128)} %all-gather.3.cloned.1.call-done, s32[32]{0:T(128)S(1)} %copy-done.4, s32[5]{0:T(128)S(1)} %fusion.59), kind=kOutput, calls=%fused_computation | convolution fusion | flops 125829280 | bytes 9699476 | tf_op jit(solution)/shard_map/aj,jxy->axy/dot_general | solution.py:45
  225.2 1.6 multiply_bitcast_fusion.1
  227.9 45.9 %psum.21 = f32[256,16]{0,1:T(8,128)S(1)} all-reduce(f32[256,16]{0,1:T(8,128)S(1)} %fusion.22), channel_id=1, replica_groups=mesh['row'=16,'col'=16] {'row'}, use_global_device_ids=true, to_apply=%region_1.0 | all-reduce | flops 4096 | bytes 32768 | tf_op jit(solution)/shard_map/psum | solution.py:58
  276.3 32.7 %collective-permute-done.4 = f32[6,256,256]{1,2,0:T(8,128)S(1)} collective-permute-done((f32[6,256,256]{1,2,0:T(8,128)S(1)}, f32[6,256,256]{1,2,0:T(8,128)S(1)}, u32[]{:S(2)}, u32[]{:S(2)}) %collective-permute-start.4) | collective-permute-done | bytes 1572896 | tf_op jit(solution)/shard_map/ppermute | solution.py:13
  309.2 3.8 collective-permute-start.5
  313.0 30.7 %collective-permute-done.5 = f32[6,256,256]{1,2,0:T(8,128)S(1)} collective-permute-done((f32[6,256,256]{1,2,0:T(8,128)S(1)}, f32[6,256,256]{1,2,0:T(8,128)S(1)}, u32[]{:S(2)}, u32[]{:S(2)}) %collective-permute-start.5) | collective-permute-done | bytes 1572896 | tf_op jit(solution)/shard_map/ppermute | solution.py:13
  345.4 31.3 %collective-permute-done.6 = f32[6,256,256]{1,2,0:T(8,128)S(1)} collective-permute-done((f32[6,256,256]{1,2,0:T(8,128)S(1)}, f32[6,256,256]{1,2,0:T(8,128)S(1)}, u32[]{:S(2)}, u32[]{:S(2)}) %collective-permute-start.6) | collective-permute-done | bytes 1572896 | tf_op jit(solution)/shard_map/ppermute | solution.py:13
  377.0 3.9 collective-permute-start.7
  381.2 5.9 %fusion.8 = f32[5,256,256]{2,0,1:T(8,128)S(1)} fusion(f32[16,256,256]{2,1,0:T(8,128)} %all-gather.5.cloned.1.call-done, s32[16]{0:T(128)S(1)} %copy-done.5, s32[5]{0:T(128)S(1)} %fusion.59), kind=kOutput, calls=%fused_computation.8 | convolution fusion | flops 62914640 | bytes 5505108 | tf_op jit(solution)/shard_map/aj,jxy->axy/dot_general | solution.py:45
  387.2 2.3 fusion.27
  389.5 22.2 %collective-permute-done.7 = f32[6,256,256]{1,2,0:T(8,128)} collective-permute-done((f32[6,256,256]{1,2,0:T(8,128)S(1)}, f32[6,256,256]{1,2,0:T(8,128)}, u32[]{:S(2)}, u32[]{:S(2)}) %collective-permute-start.7) | collective-permute-done | bytes 1572896 | tf_op jit(solution)/shard_map/ppermute | solution.py:13
  413.6 54.8 %all-reduce = (f32[16,16,16]{0,2,1:T(8,128)S(1)}, f32[256,16]{0,1:T(8,128)S(1)}) all-reduce(f32[16,16,16]{0,2,1:T(8,128)S(1)} %bitcast.79, f32[256,16]{0,1:T(8,128)S(1)} %convolution_bitcast_fusion.1), channel_id=1, replica_groups=mesh['row'=16,'col'=16] {'row'}, use_global_device_ids=true, to_apply=%region_3.0 | all-reduce | flops 8192 | bytes 65536 | tf_op jit(solution)/shard_map/psum | solution.py:77
  469.2 7.3 %all-to-all-start = ((f32[16,1,256]{2,1,0:T(1,128)}), f32[16,1,256]{2,1,0:T(1,128)S(1)}, u32[]{:S(2)}, u32[]{:S(2)}) async-start(f32[16,1,256]{2,1,0:T(1,128)} %reshape.57), calls=%async_computation | async-start | bytes 32768 | tf_op jit(solution)/shard_map/all_to_all | solution.py:78
  477.2 5.5 %all-to-all-done = f32[16,1,256]{2,1,0:T(1,128)S(1)} async-done(((f32[16,1,256]{2,1,0:T(1,128)}), f32[16,1,256]{2,1,0:T(1,128)S(1)}, u32[]{:S(2)}, u32[]{:S(2)}) %all-to-all-start) | async-done | bytes 16416 | tf_op jit(solution)/shard_map/all_to_all | solution.py:78
  (57 shorter events, 21.3 us)
Async XLA Ops:
  7.2 266.6 %copy-start = (f32[256,256]{1,0:T(8,128)S(1)}, f32[256,256]{1,0:T(8,128)}, u32[]{:S(2)}) copy-start(f32[256,256]{1,0:T(8,128)} %param.13) | copy-start | bytes 786436
  7.2 61.5 %all-gather.3.cloned.1.call-start = ((), (), s32[]{:S(2)}) async-start(), calls=%async_computation.1 | async-start | bytes 8912896 | tf_op jit(solution)/shard_map/all_gather | solution.py:41
  7.9 190.2 %all-gather.5.cloned.1.call-start = ((), (), s32[]{:S(2)}) async-start(), calls=%async_computation.2 | async-start | bytes 4456448 | tf_op jit(solution)/shard_map/all_gather | solution.py:41
  89.7 31.0 %collective-permute-start = (f32[5,256,256]{1,2,0:T(8,128)S(1)}, f32[5,256,256]{1,2,0:T(8,128)S(1)}, u32[]{:S(2)}, u32[]{:S(2)}) collective-permute-start(f32[5,256,256]{1,2,0:T(8,128)S(1)} %fusion.12), channel_id=1, source_target_pairs={{0,1},{1,0},{2,3},{3,2},{4,5},{5,4},{6,7},{7,6},{8,9},{9,8},{10,11... | collective-permute-start | bytes 3932168 | tf_op jit(solution)/shard_map/ppermute | solution.py:13
  120.9 45.2 %copy-start.2 = (f32[256,256]{1,0:T(8,128)S(1)}, f32[256,256]{1,0:T(8,128)}, u32[]{:S(2)}) copy-start(f32[256,256]{1,0:T(8,128)} %param.14) | copy-start | bytes 786436
  120.9 45.3 %copy-start.4 = (s32[32]{0:T(128)S(1)}, s32[32]{0:T(128)}, u32[]{:S(2)}) copy-start(s32[32]{0:T(128)} %param.9) | copy-start | bytes 388
  120.9 43.4 %collective-permute-start.1 = (f32[5,256,256]{1,2,0:T(8,128)S(1)}, f32[5,256,256]{1,2,0:T(8,128)S(1)}, u32[]{:S(2)}, u32[]{:S(2)}) collective-permute-start(f32[5,256,256]{1,2,0:T(8,128)S(1)} %add.76), channel_id=1, source_target_pairs={{0,2},{1,3},{2,0},{3,1},{4,6},{5,7},{6,4},{7,5},{8,10},{9,11},{10,... | collective-permute-start | bytes 3932168 | tf_op jit(solution)/shard_map/ppermute | solution.py:13
  164.5 29.3 %collective-permute-start.2 = (f32[5,256,256]{1,2,0:T(8,128)S(1)}, f32[5,256,256]{1,2,0:T(8,128)S(1)}, u32[]{:S(2)}, u32[]{:S(2)}) collective-permute-start(f32[5,256,256]{1,2,0:T(8,128)S(1)} %add.77), channel_id=1, source_target_pairs={{0,4},{1,5},{2,6},{3,7},{4,0},{5,1},{6,2},{7,3},{8,12},{9,13},{10,... | collective-permute-start | bytes 3932168 | tf_op jit(solution)/shard_map/ppermute | solution.py:13
  166.4 31.7 %copy-start.5 = (s32[16]{0:T(128)S(1)}, s32[16]{0:T(128)}, u32[]{:S(2)}) copy-start(s32[16]{0:T(128)} %param.10) | copy-start | bytes 196
  195.1 30.2 %collective-permute-start.3 = (f32[5,256,256]{1,2,0:T(8,128)}, f32[5,256,256]{1,2,0:T(8,128)}, u32[]{:S(2)}, u32[]{:S(2)}) collective-permute-start(f32[5,256,256]{1,2,0:T(8,128)} %add.78), channel_id=1, source_target_pairs={{0,8},{1,9},{2,10},{3,11},{4,12},{5,13},{6,14},{7,15},{8,0},{9,1},... | collective-permute-start | bytes 3932168 | tf_op jit(solution)/shard_map/ppermute | solution.py:13
  273.7 1.9 copy-start.1
  275.7 33.3 %collective-permute-start.4 = (f32[6,256,256]{1,2,0:T(8,128)S(1)}, f32[6,256,256]{1,2,0:T(8,128)S(1)}, u32[]{:S(2)}, u32[]{:S(2)}) collective-permute-start(f32[6,256,256]{1,2,0:T(8,128)S(1)} %pad_maximum_fusion), channel_id=1, source_target_pairs={{0,1},{1,0},{2,3},{3,2},{4,5},{5,4},{6,7},{7,6},{8,9},{9,8},{10,11... | collective-permute-start | bytes 4718600 | tf_op jit(solution)/shard_map/ppermute | solution.py:13
  309.2 34.4 %collective-permute-start.5 = (f32[6,256,256]{1,2,0:T(8,128)S(1)}, f32[6,256,256]{1,2,0:T(8,128)S(1)}, u32[]{:S(2)}, u32[]{:S(2)}) collective-permute-start(f32[6,256,256]{1,2,0:T(8,128)S(1)} %fusion.60), channel_id=1, source_target_pairs={{0,2},{1,3},{2,0},{3,1},{4,6},{5,7},{6,4},{7,5},{8,10},{9,11},{10,... | collective-permute-start | bytes 4718600 | tf_op jit(solution)/shard_map/ppermute | solution.py:13
  343.8 37.0 %copy-start.3 = (f32[256,256]{1,0:T(8,128)S(1)}, f32[256,256]{1,0:T(8,128)}, u32[]{:S(2)}) copy-start(f32[256,256]{1,0:T(8,128)} %param.15) | copy-start | bytes 786436
  343.9 32.9 %collective-permute-start.6 = (f32[6,256,256]{1,2,0:T(8,128)S(1)}, f32[6,256,256]{1,2,0:T(8,128)S(1)}, u32[]{:S(2)}, u32[]{:S(2)}) collective-permute-start(f32[6,256,256]{1,2,0:T(8,128)S(1)} %add.84), channel_id=1, source_target_pairs={{0,4},{1,5},{2,6},{3,7},{4,0},{5,1},{6,2},{7,3},{8,12},{9,13},{10,... | collective-permute-start | bytes 4718600 | tf_op jit(solution)/shard_map/ppermute | solution.py:13
  377.0 34.7 %collective-permute-start.7 = (f32[6,256,256]{1,2,0:T(8,128)S(1)}, f32[6,256,256]{1,2,0:T(8,128)}, u32[]{:S(2)}, u32[]{:S(2)}) collective-permute-start(f32[6,256,256]{1,2,0:T(8,128)S(1)} %add.85), channel_id=1, source_target_pairs={{0,8},{1,9},{2,10},{3,11},{4,12},{5,13},{6,14},{7,15},{8,0},{9,1},... | collective-permute-start | bytes 4718600 | tf_op jit(solution)/shard_map/ppermute | solution.py:13
  469.2 13.5 %all-to-all-start = ((f32[16,1,256]{2,1,0:T(1,128)}), f32[16,1,256]{2,1,0:T(1,128)S(1)}, u32[]{:S(2)}, u32[]{:S(2)}) async-start(f32[16,1,256]{2,1,0:T(1,128)} %reshape.57), calls=%async_computation | async-start | bytes 32768 | tf_op jit(solution)/shard_map/all_to_all | solution.py:78
Sparse Core Ops, SparseCore 0:
  9.8 58.7 all-gather.2
  70.5 40.4 all-gather.4
